TPU v7x, 128 devices: a whole 4x4x4 slice. The times are simulated.
128 devices in a mesh: dp: 4 (over y_hi, core), mp: 32 (over x, z, y_lo).
Axes of the slice: x: 4, y: 4 (y_hi: 2, y_lo: 2; y = y_hi * 2 + y_lo), z: 4, core: 2. Of those that a mesh axis runs over, the one named last changes fastest.
Arguments:
- step_ids: int32 [32, 4], P('dp'), may hold values from 0 to 31999
- prompt_lens: int32 [32], P('dp'), may hold values from 128 to 1024
- embed_table: bfloat16 [32000, 4096], P(None, 'mp'), may hold values from -170 to 170
- attn_gain: bfloat16 [4096], replicated, may hold values from 0.099609375 to 1.8984375
- w_qkv: bfloat16 [3, 4096, 4096], P(None, None, 'mp'), may hold values from -0.09375 to 0.09375
- w_out: bfloat16 [4096, 4096], P('mp'), may hold values from -0.1875 to 0.1875
- key_cache: bfloat16 [32, 32, 1024, 128], P('dp', 'mp'), may hold values from -194 to 194
- value_cache: bfloat16 [32, 32, 1024, 128], P('dp', 'mp'), may hold values from -6 to 6
- reward_pieces: bfloat16 [32, 4096, 4096], P('dp', None, 'mp'), may hold values from -170 to 170
- piece_lens: int32 [32], P('dp'), may hold values from 256 to 4096
- reward_gain: bfloat16 [4096], replicated, may hold values from 0.099609375 to 1.8984375
- w_value: bfloat16 [4096, 2048], P('mp'), may hold values from -0.09375 to 0.09375
- b_value: float32 [2048], replicated, may hold values from -4 to 4
- w_score: float32 [2048], replicated, may hold values from -0.125 to 0.125
- b_score: float32 [1], replicated, may hold values from -3 to 3
Outputs:
- attn_out: bfloat16 [32, 4, 4096], P('dp')
- piece_values: float32 [32, 4096], P('dp', 'mp')
All inputs are finite; a program needn't handle non-finite values.
Results may differ from a plain program's by a relative error of at most 0.015.
Values may be sent and summed in bfloat16 or wider, within the bound.
No kernel may reach another device: no remote copies, remote signals or barrier semaphores. Data moves between devices by JAX's collectives and lax.ppermute only.
A program may use at most 192 MiB of HBM per device.

v0:
```python
import math
import jax
import jax.numpy as jnp
from jax import lax
from jax.sharding import PartitionSpec as P

epsilon = 1e-05
masked = -1e30


def normalize(rows_in, gain_vec):
    widened = rows_in.astype(jnp.float32)
    inverse_rms = lax.rsqrt(jnp.mean(widened * widened, axis=-1, keepdims=True) + epsilon)
    return (widened * inverse_rms * gain_vec.astype(jnp.float32)).astype(jnp.bfloat16)


def rotate(vectors, positions):
    half_dim = vectors.shape[-1] // 2
    frequency = 10000.0 ** (-2.0 * jnp.arange(half_dim, dtype=jnp.float32) / (2 * half_dim))
    angles = positions.astype(jnp.float32)[:, None, None] * frequency
    cosines = jnp.cos(angles)
    sines = jnp.sin(angles)
    first_half = vectors[..., :half_dim]
    second = vectors[..., half_dim:]
    return jnp.concatenate(
        [first_half * cosines - second * sines, second * cosines + first_half * sines], axis=-1
    )


def project(normed, w_qkv, positions, head_dim):
    projected = jnp.einsum("nd,cde->nce", normed, w_qkv, preferred_element_type=jnp.float32)
    head_count = projected.shape[2] // head_dim
    projected = projected.reshape(projected.shape[0], 3, head_count, head_dim)
    queries = rotate(projected[:, 0], positions).astype(jnp.bfloat16)
    new_key = rotate(projected[:, 1], positions).astype(jnp.bfloat16)
    new_value = projected[:, 2].astype(jnp.bfloat16)
    return (queries, new_key, new_value)


def attend(queries, key_cache, value_cache, live_slots, new_keys, new_values, query_steps):
    inverse_root = 1.0 / math.sqrt(queries.shape[-1])
    cache_scores = (
        jnp.einsum("rhqd,rhld->rhql", queries, key_cache, preferred_element_type=jnp.float32)
        * inverse_root
    )
    cache_scores = jnp.where(live_slots[:, None, None, :], cache_scores, masked)
    new_scores = (
        jnp.einsum("rhqd,rhsd->rhqs", queries, new_keys, preferred_element_type=jnp.float32)
        * inverse_root
    )
    causal = jnp.arange(new_keys.shape[2], dtype=jnp.int32)[None, :] <= query_steps[:, None]
    new_scores = jnp.where(causal[None, None], new_scores, masked)
    row_max = jnp.maximum(
        jnp.max(cache_scores, axis=-1, keepdims=True), jnp.max(new_scores, axis=-1, keepdims=True)
    )
    cache_weights = jnp.exp(cache_scores - row_max)
    new_weights = jnp.exp(new_scores - row_max)
    weight_total = jnp.sum(cache_weights, axis=-1) + jnp.sum(new_weights, axis=-1)
    mixed = jnp.einsum(
        "rhql,rhld->rhqd",
        cache_weights.astype(jnp.bfloat16),
        value_cache,
        preferred_element_type=jnp.float32,
    )
    mixed = mixed + jnp.einsum(
        "rhqs,rhsd->rhqd",
        new_weights.astype(jnp.bfloat16),
        new_values,
        preferred_element_type=jnp.float32,
    )
    return (mixed / weight_total[..., None]).astype(jnp.bfloat16)


def combine_heads(partial_sum):
    return lax.psum(partial_sum, "mp").astype(jnp.bfloat16)


def per_device(
    step_ids,
    prompt_lens,
    embed_table,
    attn_gain,
    w_qkv,
    w_out,
    key_cache,
    value_cache,
    reward_pieces,
    piece_lens,
    reward_gain,
    w_value,
    b_value,
    w_score,
    b_score,
):
    row_count, step_count = step_ids.shape
    head_dim = key_cache.shape[3]
    cache_slots = jnp.arange(key_cache.shape[2], dtype=jnp.int32)
    live_slots = cache_slots[None, :] < prompt_lens[:, None]
    key_list = []
    value_list = []
    results = []
    for step_index in range(step_count):
        local_rows = jnp.take(embed_table, step_ids[:, step_index], axis=0)
        full_rows = lax.all_gather(local_rows, "mp", axis=1, tiled=True)
        normed = normalize(full_rows, attn_gain)
        queries, new_key, new_value = project(normed, w_qkv, prompt_lens + step_index, head_dim)
        key_list.append(new_key[:, :, None, :])
        value_list.append(new_value[:, :, None, :])
        head_out = attend(
            queries[:, :, None, :],
            key_cache,
            value_cache,
            live_slots,
            jnp.concatenate(key_list, axis=2),
            jnp.concatenate(value_list, axis=2),
            jnp.array([step_index], dtype=jnp.int32),
        )
        partial_sum = jnp.dot(
            head_out.reshape(row_count, -1), w_out, preferred_element_type=jnp.float32
        )
        results.append(combine_heads(partial_sum[:, None, :]))
    attn_out = jnp.concatenate(results, axis=1)
    normed_pieces = normalize(
        lax.all_to_all(reward_pieces, "mp", split_axis=1, concat_axis=2, tiled=True), reward_gain
    )
    piece_count, seq_local, model_width = normed_pieces.shape
    token_rows = normed_pieces.reshape(piece_count * seq_local, model_width)
    preact = jnp.dot(
        token_rows,
        lax.all_gather(w_value, "mp", axis=0, tiled=True),
        preferred_element_type=jnp.float32,
    )
    hidden = jax.nn.silu(preact + b_value)
    scored = jnp.dot(hidden, w_score, precision=lax.Precision.HIGHEST) + b_score[0]
    scored = scored.reshape(piece_count, seq_local)
    positions_here = lax.axis_index("mp") * seq_local + jnp.arange(seq_local, dtype=jnp.int32)
    piece_values = jnp.where(positions_here[None, :] < piece_lens[:, None], scored, 0.0)
    return (attn_out, piece_values)


def solution(mesh):
    return jax.shard_map(
        per_device,
        mesh=mesh,
        in_specs=(
            P("dp", None),
            P("dp"),
            P(None, "mp"),
            P(),
            P(None, None, "mp"),
            P("mp", None),
            P("dp", "mp", None, None),
            P("dp", "mp", None, None),
            P("dp", None, "mp"),
            P("dp"),
            P(),
            P("mp", None),
            P(),
            P(),
            P(),
        ),
        out_specs=(P("dp", None, None), P("dp", "mp")),
        check_vma=False,
    )
```

profile of v0, /device:TPU:0, one launch (start us, length us, event | category | flops | bytes accessed | tf_op | source)
XLA Modules:
  0.0 725.0 jit_solution(3366700105728323592)
XLA Ops:
  7.2 0.7 all-gather.2.cloned.1.call-update
  7.9 10.5 %copy.97 = bf16[8,4096,128]{2,0,1:T(8,128)(2,1)} copy(bf16[8,4096,128]{2,1,0:T(8,128)(2,1)} %param.29) | data formatting | bytes 16777216 | tf_op args[8]
  18.5 9.6 %all-to-all-start = ((bf16[8,4096,128]{2,0,1:T(8,128)(2,1)}), bf16[8,4096,128]{2,0,1:T(8,128)(2,1)}, u32[]{:S(2)}, u32[]{:S(2)}) async-start(bf16[8,4096,128]{2,0,1:T(8,128)(2,1)} %copy.97), calls=%async_computation | async-start | bytes 16777216 | tf_op jit(solution)/shard_map/all_to_all | solution.py:124
  28.1 5.0 gather_fusion
  33.1 4.9 gather_fusion.3
  38.0 4.9 gather_fusion.2
  43.0 4.9 gather_fusion.1
  48.0 196.1 %all_gather.15 = bf16[8,4096]{1,0:T(8,128)(2,1)S(1)} all-gather(bf16[8,128]{1,0:T(8,128)(2,1)S(1)} %broadcast_select_fusion.3), channel_id=1, replica_groups=mesh['dp'=4,'mp'=32] {'mp'}, dimensions={1}, use_global_device_ids=true | all-gather | bytes 67584 | tf_op jit(solution)/shard_map/all_gather | solution.py:104
  244.2 76.6 %all_gather.18 = bf16[8,4096]{1,0:T(8,128)(2,1)S(1)} all-gather(bf16[8,128]{1,0:T(8,128)(2,1)S(1)} %broadcast_select_fusion), channel_id=1, replica_groups=mesh['dp'=4,'mp'=32] {'mp'}, dimensions={1}, use_global_device_ids=true | all-gather | bytes 67584 | tf_op jit(solution)/shard_map/all_gather | solution.py:104
  320.9 79.8 %all_gather.17 = bf16[8,4096]{1,0:T(8,128)(2,1)S(1)} all-gather(bf16[8,128]{1,0:T(8,128)(2,1)S(1)} %broadcast_select_fusion.1), channel_id=1, replica_groups=mesh['dp'=4,'mp'=32] {'mp'}, dimensions={1}, use_global_device_ids=true | all-gather | bytes 67584 | tf_op jit(solution)/shard_map/all_gather | solution.py:104
  400.7 77.0 %all_gather.16 = bf16[8,4096]{1,0:T(8,128)(2,1)S(1)} all-gather(bf16[8,128]{1,0:T(8,128)(2,1)S(1)} %broadcast_select_fusion.2), channel_id=1, replica_groups=mesh['dp'=4,'mp'=32] {'mp'}, dimensions={1}, use_global_device_ids=true | all-gather | bytes 67584 | tf_op jit(solution)/shard_map/all_gather | solution.py:104
  477.7 0.1 fusion.31
  477.9 0.2 fusion.40
  478.1 0.5 fusion.44
  478.6 0.6 fusion.51
  479.2 0.1 fusion.182
  479.4 0.1 fusion.37
  479.5 0.1 fusion.34
  479.7 0.5 convolution_bitcast_fusion.4
  480.3 0.6 convolution_bitcast_fusion.5
  480.8 0.5 copy-done.2
  481.3 0.6 fusion.29
  481.9 0.1 fusion.190
  482.1 0.6 slice.256
  482.7 0.6 slice.259
  483.3 0.2 fusion.160
  483.5 0.2 fusion.77
  483.8 0.6 fusion.23
  484.4 0.7 fusion.25
  485.1 0.7 fusion.27
  485.7 0.2 fusion.69
  486.0 0.4 fusion.21
  486.4 0.3 convolution_bitcast_fusion.3
  486.8 0.1 fusion.164
  487.1 0.1 fusion.87
  487.3 0.1 fusion.91
  487.7 0.1 copy.114
  487.9 0.5 copy-done.12
  488.4 0.8 fusion.71
  489.2 0.1 fusion.162
  489.4 0.4 fusion.19
  489.7 0.3 convolution_bitcast_fusion.2
  490.2 0.1 copy.123
  490.3 0.1 fusion.89
  490.4 0.4 fusion.17
  490.8 0.3 convolution_bitcast_fusion.1
  491.1 1.9 fusion.197
  493.0 1.3 copy.132
  494.3 0.7 add.188
  494.9 0.7 slice_bitcast_fusion.9
  495.6 0.7 slice_bitcast_fusion.8
  496.3 0.7 maximum_bitcast_fusion.1
  497.0 0.8 fusion.85
  497.8 0.4 fusion.15
  498.1 0.3 convolution_bitcast_fusion
  498.5 158.8 %all-reduce.2 = (bf16[8,1,4096]{2,0,1:T(8,128)(2,1)S(1)}, bf16[8,1,4096]{2,0,1:T(8,128)(2,1)S(1)}, bf16[8,1,4096]{2,0,1:T(8,128)(2,1)S(1)}, bf16[8,1,4096]{2,0,1:T(8,128)(2,1)S(1)}) all-reduce(f32[8,1,4096]{2,0,1:T(8,128)S(1)} %convolution_bitcast_fusion, ...), channel_id=1, replica_groups=mesh['dp'=4,'mp'=32] {'mp'}, use_global_device_ids=true, to_apply=%region_21.23 | all-reduce | flops 131072 | bytes 786432 | tf_op jit(solution)/shard_map/psum | solution.py:75
  657.3 0.9 copy.100
  658.2 0.7 convert_element_type.246
  659.6 13.9 %copy.98 = f32[8,32,128,128]{3,1,2,0:T(8,128)} copy(bf16[8,32,128,128]{3,0,2,1:T(8,128)(2,1)} %bitcast.258) | data formatting | bytes 25165824 | tf_op jit(solution)/shard_map/convert_element_type | solution.py:12
  673.5 8.5 %multiply_reduce_fusion = f32[8,4096]{0,1:T(8,128)S(1)} fusion(bf16[8,4096,128]{2,0,1:T(8,128)(2,1)} %all-to-all-done), kind=kLoop, calls=%fused_computation.7 | loop fusion | flops 12550144 | bytes 8519680 | tf_op jit(solution)/shard_map/reduce_sum | solution.py:13
  682.1 0.2 reduce_sum.132
  682.3 26.2 %fusion.2 = f32[1024,2048]{1,0:T(8,128)S(1)} fusion(bf16[4096,2048]{1,0:T(8,128)(2,1)} %all-gather.2.cloned.1.call-done, f32[128,8,32,128]{3,2,1,0:T(8,128)} %bitcast.281, f32[4096]{0:T(1024)S(1)} %convert_element_type.246, f32[1024]{0:T(1024)S(1)} %rsqrt_bitcast_fusion), kind=kOutput, calls=%fused_computation.8 | convolution fusion | flops 17192452096 | bytes 41963520 | tf_op jit(solution)/shard_map/dot_general | solution.py:128
  708.6 8.8 %fusion.4 = f32[1,1024]{1,0:T(1,128)S(1)} fusion(f32[2048,1]{0,1:T(1,128)S(1)} %bitcast.306, f32[1024,2048]{1,0:T(8,128)S(1)} %fusion.2, f32[2048]{0:T(1024)S(1)} %copy-done.15), kind=kOutput, calls=%fused_computation.9 | convolution fusion | flops 35651584 | bytes 8409088 | tf_op jit(solution)/shard_map/dot_general | solution.py:134
  717.4 0.7 bitcast_select_fusion
  (86 shorter events, 1.7 us)
Async XLA Ops:
  7.2 470.9 %copy-start = (bf16[3,4096,128]{2,1,0:T(8,128)(2,1)S(1)}, bf16[3,4096,128]{2,1,0:T(8,128)(2,1)}, u32[]{:S(2)}) copy-start(bf16[3,4096,128]{2,1,0:T(8,128)(2,1)} %param.25) | copy-start | bytes 9437188
  7.2 675.1 %all-gather.2.cloned.1.call-start = ((), (), s32[]{:S(2)}) async-start(), calls=%async_computation.1 | async-start | bytes 17301504 | tf_op jit(solution)/shard_map/all_gather | solution.py:130
  18.5 9.6 %copy-start.9 = (bf16[4096]{0:T(1024)(128)(2,1)S(1)}, bf16[4096]{0:T(1024)(128)(2,1)}, u32[]{:S(2)}) copy-start(bf16[4096]{0:T(1024)(128)(2,1)} %param.24) | copy-start | bytes 24580
  18.5 9.6 %copy-start.11 = (s32[8,4]{0,1:T(4,128)S(1)}, s32[8,4]{0,1:T(4,128)}, u32[]{:S(2)}) copy-start(s32[8,4]{0,1:T(4,128)} %param.21) | copy-start | bytes 388
  18.5 459.6 %copy-start.8 = (s32[8]{0:T(128)S(1)}, s32[8]{0:T(128)}, u32[]{:S(2)}) copy-start(s32[8]{0:T(128)} %param.22) | copy-start | bytes 100
  18.5 641.1 %all-to-all-start = ((bf16[8,4096,128]{2,0,1:T(8,128)(2,1)}), bf16[8,4096,128]{2,0,1:T(8,128)(2,1)}, u32[]{:S(2)}, u32[]{:S(2)}) async-start(bf16[8,4096,128]{2,0,1:T(8,128)(2,1)} %copy.97), calls=%async_computation | async-start | bytes 16777216 | tf_op jit(solution)/shard_map/all_to_all | solution.py:124
  479.7 1.6 copy-start.2
  480.3 3.5 copy-start.5
  480.8 2.9 copy-start.6
  483.7 2.2 copy-start.3
  484.4 2.0 copy-start.4
  487.3 1.2 copy-start.7
  487.8 0.5 copy-start.12
  488.3 0.9 copy-start.10
  682.3 26.3 %copy-start.14 = (f32[2048]{0:T(1024)S(1)}, f32[2048]{0:T(1024)}, u32[]{:S(2)}) copy-start(f32[2048]{0:T(1024)} %param.34) | copy-start | bytes 24580
  682.3 26.3 %copy-start.15 = (f32[2048]{0:T(1024)S(1)}, f32[2048]{0:T(1024)}, u32[]{:S(2)}) copy-start(f32[2048]{0:T(1024)} %param.33) | copy-start | bytes 24580
  708.6 8.9 %copy-start.13 = (s32[8]{0:T(128)S(1)}, s32[8]{0:T(128)}, u32[]{:S(2)}) copy-start(s32[8]{0:T(128)} %param.30) | copy-start | bytes 100
  708.6 9.5 %copy-start.1 = (bf16[3,4096,128]{2,1,0:T(8,128)(2,1)S(1)}, bf16[3,4096,128]{2,1,0:T(8,128)(2,1)}, u32[]{:S(2)}) copy-start(bf16[3,4096,128]{2,1,0:T(8,128)(2,1)} %param.25) | copy-start | bytes 9437188
Sparse Core Ops, SparseCore 0:
  9.6 472.2 all-gather.1
where the time goes:
time: 726 us; the launch traced here: 725 us
  blocking collectives  588 us (81%)
  local copies, waits for them, and re-layouts  50.6 us (7%)
  matrix products  44 us (6%)
  other arithmetic  16.8 us (2%)
  between operations  15 us (2%)
  starting transfers between devices  9.59 us (1%)
    all_gather x4, blocking collectives, per_device(): full_rows = lax.all_gather(local_rows, 'mp', axis=1, tiled=True)  429 us
    psum x1, blocking collectives, combine_heads(): return lax.psum(partial_sum, 'mp').astype(jnp.bfloat16)  159 us
    dot_general x1, matrix products, per_device(): jnp.dot(token_rows, lax.all_gather(w_value, 'mp', axis=0, tiled=True), pr...  26.2 us
    gather x4, local copies, waits for them, and re-layouts, per_device(): local_rows = jnp.take(embed_table, step_ids[:, step_index], axis=0)  19.8 us
  transfers between devices with their start and end apart: 2, of which 0 were waited for; matrix products, arithmetic and copies ran while one was open for 10% of the time, Pallas kernels for 0%

commit v1 on v0

--- a/solution.py
+++ b/solution.py
@@ -101,7 +101,15 @@
     results = []
     for step_index in range(step_count):
         local_rows = jnp.take(embed_table, step_ids[:, step_index], axis=0)
-        full_rows = lax.all_gather(local_rows, "mp", axis=1, tiled=True)
+        full_rows = jnp.concatenate(
+            lax.all_to_all(
+                jnp.stack([local_rows for _ in range(lax.axis_size("mp"))]),
+                split_axis=0,
+                concat_axis=0,
+                axis_name="mp",
+            ),
+            1,
+        )
         normed = normalize(full_rows, attn_gain)
         queries, new_key, new_value = project(normed, w_qkv, prompt_lens + step_index, head_dim)
         key_list.append(new_key[:, :, None, :])

time: 726 us -> 549 us (0.76)
  blocking collectives: 588 us -> 282 us
  waiting for transfers between devices: 0.69 us -> 99.7 us
  starting transfers between devices: 9.59 us -> 30.5 us
    all_gather x4 -> x0, blocking collectives: 429 us -> none  [per_device(): full_rows = lax.all_gather(local_rows, 'mp', axis=1, tiled=True)]
    psum x1, blocking collectives: 159 us -> 282 us  [combine_heads(): return lax.psum(partial_sum, 'mp').astype(jnp.bfloat16)]
    all_gather x1, waiting for transfers between devices: 0.01 us -> 74.5 us  [per_device(): lax.all_gather(w_value, 'mp', axis=0, tiled=True)]
    all_to_all x0 -> x4, starting transfers between devices: none -> 25.3 us  [per_device(): lax.all_to_all(jnp.stack([local_rows for _ in range(lax.axis_size('mp'))]...]
    all_to_all x0 -> x4, waiting for transfers between devices: none -> 24.4 us  [per_device(): lax.all_to_all(jnp.stack([local_rows for _ in range(lax.axis_size('mp'))]...]
  transfers between devices with their start and end apart: 2 -> 6, of which waited for: 0 -> 4; matrix products, arithmetic and copies ran while one was open for 10% -> 15% of each run, Pallas kernels for 0% -> 0%
where the time goes in v1:
time: 549 us; the launch traced here: 542 us
  blocking collectives  282 us (51%)
  waiting for transfers between devices  99.7 us (18%)
  local copies, waits for them, and re-layouts  52.2 us (10%)
  matrix products  44.1 us (8%)
  starting transfers between devices  30.5 us (6%)
  other arithmetic  18.8 us (3%)
  between operations  15.1 us (3%)
    psum x1, blocking collectives, combine_heads(): return lax.psum(partial_sum, 'mp').astype(jnp.bfloat16)  282 us
    all_gather x1, waiting for transfers between devices, per_device(): lax.all_gather(w_value, 'mp', axis=0, tiled=True)  74.5 us
    dot_general x1, matrix products, per_device(): jnp.dot(token_rows, lax.all_gather(w_value, 'mp', axis=0, tiled=True), pr...  26.2 us
    all_to_all x4, starting transfers between devices, per_device(): lax.all_to_all(jnp.stack([local_rows for _ in range(lax.axis_size('mp'))]...  25.3 us
    all_to_all x4, waiting for transfers between devices, per_device(): lax.all_to_all(jnp.stack([local_rows for _ in range(lax.axis_size('mp'))]...  24.4 us
    gather x4, local copies, waits for them, and re-layouts, per_device(): local_rows = jnp.take(embed_table, step_ids[:, step_index], axis=0)  19.9 us
    convert_element_type x1, local copies, waits for them, and re-layouts, normalize(): widened = rows_in.astype(jnp.float32)  14 us
    unnamed x42, local copies, waits for them, and re-layouts  11.4 us
  transfers between devices with their start and end apart: 6, of which 4 were waited for; matrix products, arithmetic and copies ran while one was open for 15% of the time, Pallas kernels for 0%

profile of v1, /device:TPU:0, one launch (start us, length us, event | category | flops | bytes accessed | tf_op | source)
XLA Modules:
  0.0 542.1 jit_solution(7642766988164530375)
XLA Ops:
  7.2 0.7 all-gather.2.cloned.1.call-update
  7.9 0.9 compare_and_fusion.2
  8.9 4.9 gather_fusion
  13.9 0.6 stack.8
  14.5 9.3 %all-to-all-start = ((bf16[32,8,128]{2,1,0:T(8,128)(2,1)}), bf16[32,8,128]{2,1,0:T(8,128)(2,1)S(1)}, u32[]{:S(2)}, u32[]{:S(2)}) async-start(bf16[32,8,128]{2,1,0:T(8,128)(2,1)} %stack.8), calls=%async_computation | async-start | bytes 131072 | tf_op jit(solution)/shard_map/all_to_all | solution.py:105
  23.8 0.7 convert_element_type.256
  24.5 4.9 gather_fusion.3
  29.5 5.0 gather_fusion.2
  34.5 5.0 gather_fusion.1
  39.6 10.4 %copy.97 = bf16[8,4096,128]{2,0,1:T(8,128)(2,1)} copy(bf16[8,4096,128]{2,1,0:T(8,128)(2,1)} %param.29) | data formatting | bytes 16777216 | tf_op args[8]
  49.9 0.6 convert_element_type.298
  51.5 0.6 iota_add_fusion
  52.0 0.6 stack.11
  52.7 8.3 %all-to-all-start.3 = ((bf16[32,8,128]{2,1,0:T(8,128)(2,1)}), bf16[32,8,128]{2,1,0:T(8,128)(2,1)S(1)}, u32[]{:S(2)}, u32[]{:S(2)}) async-start(bf16[32,8,128]{2,1,0:T(8,128)(2,1)} %stack.11), calls=%async_computation.3 | async-start | bytes 131072 | tf_op jit(solution)/shard_map/all_to_all | solution.py:105
  61.0 0.1 fusion.34
  61.1 8.1 %all-to-all-done.3 = bf16[32,8,128]{2,1,0:T(8,128)(2,1)S(1)} async-done(((bf16[32,8,128]{2,1,0:T(8,128)(2,1)}), bf16[32,8,128]{2,1,0:T(8,128)(2,1)S(1)}, u32[]{:S(2)}, u32[]{:S(2)}) %all-to-all-start.3) | async-done | bytes 65568 | tf_op jit(solution)/shard_map/all_to_all | solution.py:105
  69.3 0.6 stack.10
  69.9 3.9 all-to-all-start.2
  73.8 0.1 fusion.46
  74.0 8.1 %all-to-all-done.2 = bf16[32,8,128]{2,1,0:T(8,128)(2,1)S(1)} async-done(((bf16[32,8,128]{2,1,0:T(8,128)(2,1)}), bf16[32,8,128]{2,1,0:T(8,128)(2,1)S(1)}, u32[]{:S(2)}, u32[]{:S(2)}) %all-to-all-start.2) | async-done | bytes 65568 | tf_op jit(solution)/shard_map/all_to_all | solution.py:105
  82.1 0.6 stack.9
  82.7 3.9 all-to-all-start.1
  86.6 0.1 fusion.42
  86.7 8.2 %all-to-all-done.1 = bf16[32,8,128]{2,1,0:T(8,128)(2,1)S(1)} async-done(((bf16[32,8,128]{2,1,0:T(8,128)(2,1)}), bf16[32,8,128]{2,1,0:T(8,128)(2,1)S(1)}, u32[]{:S(2)}, u32[]{:S(2)}) %all-to-all-start.1) | async-done | bytes 65568 | tf_op jit(solution)/shard_map/all_to_all | solution.py:105
  94.9 5.2 all-to-all-start.4
  100.1 0.1 fusion.38
  100.3 0.5 fusion.48
  100.8 0.6 fusion.55
  101.4 0.6 convolution_bitcast_fusion.4
  102.0 0.6 convolution_bitcast_fusion.5
  102.7 0.6 slice.256
  103.3 0.6 slice.259
  103.9 0.2 fusion.164
  104.3 0.6 fusion.29
  104.9 0.2 fusion.81
  105.2 0.6 fusion.23
  105.8 0.7 fusion.25
  106.5 0.7 fusion.27
  107.1 0.2 fusion.73
  107.4 0.4 fusion.21
  107.8 0.3 convolution_bitcast_fusion.3
  109.4 0.7 fusion.75
  110.2 0.4 fusion.19
  110.6 0.3 convolution_bitcast_fusion.2
  111.3 0.4 fusion.17
  111.7 0.3 convolution_bitcast_fusion.1
  112.0 1.9 fusion.201
  113.8 1.3 copy.132
  115.1 0.7 add.188
  115.8 0.7 slice_bitcast_fusion.9
  116.5 0.7 slice_bitcast_fusion.8
  117.2 0.7 maximum_bitcast_fusion.1
  117.8 0.8 fusion.89
  118.6 0.4 fusion.15
  119.0 0.3 convolution_bitcast_fusion
  119.3 281.8 %all-reduce.2 = (bf16[8,1,4096]{2,0,1:T(8,128)(2,1)S(1)}, bf16[8,1,4096]{2,0,1:T(8,128)(2,1)S(1)}, bf16[8,1,4096]{2,0,1:T(8,128)(2,1)S(1)}, bf16[8,1,4096]{2,0,1:T(8,128)(2,1)S(1)}) all-reduce(f32[8,1,4096]{2,0,1:T(8,128)S(1)} %convolution_bitcast_fusion, ...), channel_id=1, replica_groups=mesh['dp'=4,'mp'=32] {'mp'}, use_global_device_ids=true, to_apply=%region_21.23 | all-reduce | flops 131072 | bytes 786432 | tf_op jit(solution)/shard_map/psum | solution.py:75
  401.2 0.9 copy.100
  402.1 14.0 %copy.98 = f32[8,32,128,128]{3,1,2,0:T(8,128)} copy(bf16[8,32,128,128]{3,0,2,1:T(8,128)(2,1)} %bitcast.310) | data formatting | bytes 25165824 | tf_op jit(solution)/shard_map/convert_element_type | solution.py:12
  416.1 8.5 %multiply_reduce_fusion = f32[8,4096]{0,1:T(8,128)S(1)} fusion(bf16[8,4096,128]{2,0,1:T(8,128)(2,1)} %all-to-all-done.4), kind=kLoop, calls=%fused_computation.7 | loop fusion | flops 12550144 | bytes 8519680 | tf_op jit(solution)/shard_map/reduce_sum | solution.py:13
  424.6 0.2 reduce_sum.132
  424.9 74.5 %all-gather.2.cloned.1.call-done = bf16[4096,2048]{1,0:T(8,128)(2,1)} async-done(((bf16[128,2048]{1,0:T(8,128)(2,1)}), bf16[4096,2048]{1,0:T(8,128)(2,1)}) %all-gather.2.cloned.1.call-update) | async-done | bytes 16777232 | tf_op jit(solution)/shard_map/all_gather | solution.py:138
  499.4 26.2 %fusion.2 = f32[1024,2048]{1,0:T(8,128)S(1)} fusion(bf16[4096,2048]{1,0:T(8,128)(2,1)} %all-gather.2.cloned.1.call-done, f32[128,8,32,128]{3,2,1,0:T(8,128)} %bitcast.333, f32[4096]{0:T(1024)S(1)} %copy-done.8, f32[1024]{0:T(1024)S(1)} %rsqrt_bitcast_fusion), kind=kOutput, calls=%fused_computation.8 | convolution fusion | flops 17192452096 | bytes 41963520 | tf_op jit(solution)/shard_map/dot_general | solution.py:136
  525.7 8.8 %fusion.4 = f32[1,1024]{1,0:T(1,128)S(1)} fusion(f32[2048,1]{0,1:T(1,128)S(1)} %bitcast.358, f32[1024,2048]{1,0:T(8,128)S(1)} %fusion.2, f32[2048]{0:T(1024)S(1)} %copy-done.19), kind=kOutput, calls=%fused_computation.9 | convolution fusion | flops 35651584 | bytes 8409088 | tf_op jit(solution)/shard_map/dot_general | solution.py:142
  534.6 0.7 bitcast_select_fusion
  (102 shorter events, 2.8 us)
Async XLA Ops:
  7.2 93.1 %copy-start = (bf16[3,4096,128]{2,1,0:T(8,128)(2,1)S(1)}, bf16[3,4096,128]{2,1,0:T(8,128)(2,1)}, u32[]{:S(2)}) copy-start(bf16[3,4096,128]{2,1,0:T(8,128)(2,1)} %param.25) | copy-start | bytes 9437188
  7.2 492.2 %all-gather.2.cloned.1.call-start = ((), (), s32[]{:S(2)}) async-start(), calls=%async_computation.5 | async-start | bytes 17301504 | tf_op jit(solution)/shard_map/all_gather | solution.py:138
  14.5 37.5 %all-to-all-start = ((bf16[32,8,128]{2,1,0:T(8,128)(2,1)}), bf16[32,8,128]{2,1,0:T(8,128)(2,1)S(1)}, u32[]{:S(2)}, u32[]{:S(2)}) async-start(bf16[32,8,128]{2,1,0:T(8,128)(2,1)} %stack.8), calls=%async_computation | async-start | bytes 131072 | tf_op jit(solution)/shard_map/all_to_all | solution.py:105
  39.5 10.4 %copy-start.11 = (bf16[4096]{0:T(1024)(128)(2,1)S(1)}, bf16[4096]{0:T(1024)(128)(2,1)}, u32[]{:S(2)}) copy-start(bf16[4096]{0:T(1024)(128)(2,1)} %param.31) | copy-start | bytes 24580
  39.5 11.7 %copy-start.9 = (s32[8]{0:T(128)S(1)}, s32[8]{0:T(128)}, u32[]{:S(2)}) copy-start(s32[8]{0:T(128)} %param.22) | copy-start | bytes 100
  51.2 58.0 %copy-start.13 = (pred[4]{0:T(512)(128)(4,1)}, pred[4]{0:T(512)(128)(4,1)S(1)}, u32[]{:S(2)}) copy-start(pred[4]{0:T(512)(128)(4,1)S(1)} %iota_compare_fusion.1) | copy-start | bytes 16
  51.2 58.0 %copy-start.14 = (pred[3]{0:T(512)(128)(4,1)}, pred[3]{0:T(512)(128)(4,1)S(1)}, u32[]{:S(2)}) copy-start(pred[3]{0:T(512)(128)(4,1)S(1)} %iota_compare_fusion.2) | copy-start | bytes 13
  52.7 16.6 %all-to-all-start.3 = ((bf16[32,8,128]{2,1,0:T(8,128)(2,1)}), bf16[32,8,128]{2,1,0:T(8,128)(2,1)S(1)}, u32[]{:S(2)}, u32[]{:S(2)}) async-start(bf16[32,8,128]{2,1,0:T(8,128)(2,1)} %stack.11), calls=%async_computation.3 | async-start | bytes 131072 | tf_op jit(solution)/shard_map/all_to_all | solution.py:105
  69.9 12.2 %all-to-all-start.2 = ((bf16[32,8,128]{2,1,0:T(8,128)(2,1)}), bf16[32,8,128]{2,1,0:T(8,128)(2,1)S(1)}, u32[]{:S(2)}, u32[]{:S(2)}) async-start(bf16[32,8,128]{2,1,0:T(8,128)(2,1)} %stack.10), calls=%async_computation.2 | async-start | bytes 131072 | tf_op jit(solution)/shard_map/all_to_all | solution.py:105
  82.7 12.2 %all-to-all-start.1 = ((bf16[32,8,128]{2,1,0:T(8,128)(2,1)}), bf16[32,8,128]{2,1,0:T(8,128)(2,1)S(1)}, u32[]{:S(2)}, u32[]{:S(2)}) async-start(bf16[32,8,128]{2,1,0:T(8,128)(2,1)} %stack.9), calls=%async_computation.1 | async-start | bytes 131072 | tf_op jit(solution)/shard_map/all_to_all | solution.py:105
  94.9 307.2 %all-to-all-start.4 = ((bf16[8,4096,128]{2,0,1:T(8,128)(2,1)}), bf16[8,4096,128]{2,0,1:T(8,128)(2,1)}, u32[]{:S(2)}, u32[]{:S(2)}) async-start(bf16[8,4096,128]{2,0,1:T(8,128)(2,1)} %copy.97), calls=%async_computation.4 | async-start | bytes 16777216 | tf_op jit(solution)/shard_map/all_to_all | solution.py:132
  101.4 2.9 copy-start.2
  102.0 2.3 copy-start.5
  102.5 3.9 copy-start.6
  105.2 2.2 copy-start.3
  105.8 2.0 copy-start.4
  106.5 2.9 copy-start.10
  108.7 0.7 copy-start.7
  109.3 0.8 copy-start.12
  109.4 1.6 copy-start.15
  416.1 83.3 %copy-start.8 = (f32[4096]{0:T(1024)S(1)}, f32[4096]{0:T(1024)}, u32[]{:S(2)}) copy-start(f32[4096]{0:T(1024)} %convert_element_type.298) | copy-start | bytes 49156
  499.4 26.2 %copy-start.18 = (f32[2048]{0:T(1024)S(1)}, f32[2048]{0:T(1024)}, u32[]{:S(2)}) copy-start(f32[2048]{0:T(1024)} %param.34) | copy-start | bytes 24580
  499.4 26.3 %copy-start.19 = (f32[2048]{0:T(1024)S(1)}, f32[2048]{0:T(1024)}, u32[]{:S(2)}) copy-start(f32[2048]{0:T(1024)} %param.33) | copy-start | bytes 24580
  525.7 8.9 %copy-start.16 = (s32[8]{0:T(128)S(1)}, s32[8]{0:T(128)}, u32[]{:S(2)}) copy-start(s32[8]{0:T(128)} %param.30) | copy-start | bytes 100
  525.7 8.9 %copy-start.17 = (s32[128]{0:T(128)S(1)}, s32[128]{0:T(128)}, u32[]{:S(2)}) copy-start(s32[128]{0:T(128)} %iota_add_fusion) | copy-start | bytes 1540
  525.7 9.5 %copy-start.1 = (bf16[3,4096,128]{2,1,0:T(8,128)(2,1)S(1)}, bf16[3,4096,128]{2,1,0:T(8,128)(2,1)}, u32[]{:S(2)}) copy-start(bf16[3,4096,128]{2,1,0:T(8,128)(2,1)} %param.25) | copy-start | bytes 9437188
Sparse Core Ops, SparseCore 0:
  9.6 489.7 all-gather.1
